TPU v7x, 32 devices: a whole 2x2x4 slice. The times are simulated.
32 devices in a mesh: virt: 8 (over y, x, core), occ: 4 (over z).
Axes of the slice: x: 2, y: 2, z: 4, core: 2. Of those that a mesh axis runs over, the one named last changes fastest.
Arguments:
- amplitudes: bfloat16 [512, 4096], P('occ', 'virt'), may hold values from -6 to 6
- integrals: bfloat16 [1024, 16384], P(None, 'virt'), may hold values from -0.1875 to 0.1875
- panel_owner: int32 [4, 2], P('occ'), may hold values from 0 to 7, as said below
- inter: bfloat16 [8192, 8192], P('occ', 'virt'), may hold values from -0.125 to 0.125
- dest: int32 [4, 8, 16], P('occ', 'virt'), may hold values from 0 to 3, as said below
- screen: int32 [4, 8, 16], P('occ', 'virt'), may hold values from 0 to 1
Outputs:
- contracted: bfloat16 [512, 8192], P('occ', 'virt')
Inputs may be any that keep to these rules, and one draw needn't show every extreme that they name: `panel_owner`: in each row the 2 entries are distinct. `dest`: among the subtiles of one device that screen marks 1, no two name the same owner.
All inputs are finite; a program needn't handle non-finite values.
Results may differ from a plain program's by a relative error of at most 0.0055.
Values may be sent and summed in bfloat16 or wider, within the bound.
A program may use at most 64 MiB of HBM per device.

v0:
```python
import jax
import jax.numpy as jnp
from jax import lax
from jax.sharding import PartitionSpec as P

SROWS = 32


def on_device(amplitudes, integrals, panel_owner, inter, dest, screen):
    op_rows = amplitudes.shape[0]
    tile = amplitudes.shape[1]
    cols = integrals.shape[1]
    steps = panel_owner.shape[1]
    n_sub = dest.shape[2]
    n_occ = lax.axis_size("occ")
    half_splits = op_rows // SROWS
    col_tiles = cols // tile
    every = lax.all_gather(amplitudes[None], "virt", axis=0, tiled=True)
    chosen_entries = jnp.take(every, panel_owner[0], axis=0)
    chosen_entries = chosen_entries.transpose(1, 0, 2).reshape(op_rows, steps * tile)
    accum = jnp.dot(chosen_entries, integrals, preferred_element_type=jnp.float32)
    ladder = accum.astype(jnp.bfloat16)
    subtiles = (
        ladder.reshape(half_splits, SROWS, col_tiles, tile)
        .transpose(0, 2, 1, 3)
        .reshape(n_sub, SROWS, tile)
    )
    owners = jnp.arange(n_occ, dtype=jnp.int32)
    labels = jnp.arange(1, n_sub + 1, dtype=jnp.int32)
    routing = (dest[0, 0][None, :] == owners[:, None]) & (screen[0, 0][None, :] == 1)
    outgoing = jnp.einsum(
        "os,srt->ort", routing.astype(jnp.bfloat16), subtiles, preferred_element_type=jnp.float32
    ).astype(jnp.bfloat16)
    output_marker = jnp.sum(routing.astype(jnp.int32) * labels[None, :], axis=1).astype(
        jnp.bfloat16
    )[:, None]
    arriving_tiles, tag_in = (
        lax.all_to_all(outgoing, "occ", split_axis=0, concat_axis=0, tiled=True),
        lax.all_to_all(output_marker, "occ", split_axis=0, concat_axis=0, tiled=True),
    )
    choose_surviving = tag_in.astype(jnp.float32) == labels[None, :].astype(jnp.float32)
    summed = jnp.einsum(
        "ez,ead->zad",
        choose_surviving.astype(jnp.bfloat16),
        arriving_tiles,
        preferred_element_type=jnp.float32,
    )
    gathered = summed.astype(jnp.bfloat16)
    left = (
        gathered.reshape(half_splits, col_tiles, SROWS, tile)
        .transpose(0, 2, 1, 3)
        .reshape(op_rows, cols)
    )
    return jnp.dot(left, inter, preferred_element_type=jnp.float32).astype(jnp.bfloat16)


def solution(mesh):
    return jax.shard_map(
        on_device,
        mesh=mesh,
        in_specs=(
            P("occ", "virt"),
            P(None, "virt"),
            P("occ", None),
            P("occ", "virt"),
            P("occ", "virt", None),
            P("occ", "virt", None),
        ),
        out_specs=P("occ", "virt"),
        check_vma=False,
    )
```

profile of v0, /device:TPU:0, one launch (start us, length us, event | category | flops | bytes accessed | tf_op | source)
XLA Modules:
  0.0 64.2 jit_solution(17440745688563391463)
XLA Ops:
  6.5 0.7 %all-gather.3.cloned.1.call-update = ((bf16[128,512]{1,0:T(8,128)(2,1)}), bf16[1024,512]{1,0:T(8,128)(2,1)}) async-update(((), (), s32[]{:S(2)}) %all-gather.3.cloned.1.call-start, bf16[128,512]{1,0:T(8,128)(2,1)} %param.6) | async-update | bytes 1310744
  7.3 0.7 %compare_bitcast_fusion = pred[16]{0:T(512)(128)(4,1)S(1)} fusion(s32[1,1,16]{2,1,0:T(1,128)} %param.11), kind=kLoop, calls=%fused_computation.19 | loop fusion | flops 16 | bytes 80 | tf_op jit(solution)/shard_map/eq | solution.py:30
  7.9 0.8 %select_reduce_fusion = s32[4]{0:T(128)S(1)} fusion(s32[16]{0:T(128)S(1)} %iota_add_fusion, s32[16]{0:T(128)} %bitcast.39, pred[16]{0:T(512)(128)(4,1)S(1)} %compare_bitcast_fusion), kind=kLoop, calls=%fused_computation.12 | loop fusion | flops 252 | bytes 160 | tf_op jit(solution)/shard_map/reduce_sum | solution.py:34
  8.7 0.7 %copy.20 = bf16[4,1,1]{2,1,0:T(2,128)(2,1)} copy(bf16[4,1,1]{0,2,1:T(2,128)(2,1)S(1)} %convert_bitcast_fusion) | data formatting | bytes 16 | tf_op jit(solution)/shard_map/convert_element_type | solution.py:34
  9.4 6.3 %all-to-all-start = ((bf16[4,1,1]{2,1,0:T(2,128)(2,1)}), bf16[4,1,1]{2,1,0:T(2,128)(2,1)S(1)}, u32[]{:S(2)}, u32[]{:S(2)}) async-start(bf16[4,1,1]{2,1,0:T(2,128)(2,1)} %copy.20), calls=%async_computation | async-start | bytes 4096 | tf_op jit(solution)/shard_map/all_to_all | solution.py:39
  15.7 0.7 %fusion.11 = s32[2]{0:T(128)S(1)} fusion(s32[1,2]{1,0:T(1,128)} %param.8), kind=kLoop, calls=%fused_computation.24 | loop fusion | flops 6 | bytes 16 | tf_op jit(solution)/shard_map/jit(_take)/jit(_where)/select_n | solution.py:19
  16.4 0.7 %compare_and_fusion = pred[2]{0:T(512)(128)(4,1)S(1)} fusion(s32[1,2]{1,0:T(1,128)} %param.8), kind=kLoop, calls=%fused_computation.17 | loop fusion | flops 12 | bytes 10 | tf_op jit(solution)/shard_map/jit(_take)/and | solution.py:19
  17.1 18.3 %all-gather.3.cloned.1.call-done = bf16[1024,512]{1,0:T(8,128)(2,1)} async-done(((bf16[128,512]{1,0:T(8,128)(2,1)}), bf16[1024,512]{1,0:T(8,128)(2,1)}) %all-gather.3.cloned.1.call-update) | async-done | bytes 1048592 | tf_op jit(solution)/shard_map/all_gather | solution.py:18
  35.3 1.8 %gather_fusion = bf16[2,128,512]{2,1,0:T(8,128)(2,1)S(1)} fusion(bf16[8,128,512]{2,1,0:T(8,128)(2,1)} %bitcast.38, s32[1024]{0:T(1024)S(1)} %pad_clamp_fusion), kind=kCustom, calls=%fused_computation | custom fusion | bytes 524296 | tf_op jit(solution)/shard_map/jit(_take)/gather | solution.py:19
  37.2 0.1 select_bitcast_fusion
  37.2 0.2 copy.21
  37.4 2.9 %convolution_convert_fusion = bf16[128,2048]{1,0:T(8,128)(2,1)S(1)} fusion(bf16[128,1024]{0,1:T(8,128)(2,1)S(1)} %bitcast.37, bf16[1024,2048]{1,0:T(8,128)(2,1)} %param.7), kind=kOutput, calls=%fused_computation.1 | convolution fusion | flops 537133056 | bytes 4980736 | tf_op jit(solution)/shard_map/dot_general | solution.py:21
  40.4 0.4 reshape.88
  40.7 0.1 copy.22
  40.9 0.4 convolution_convert_fusion.3
  41.3 0.7 %copy.24 = bf16[4,32,512]{2,1,0:T(8,128)(2,1)} copy(bf16[4,32,512]{2,0,1:T(4,128)(2,1)S(1)} %convolution_convert_fusion.3) | data formatting | bytes 262144 | tf_op jit(solution)/shard_map/convert_element_type | solution.py:33
  41.9 4.6 %all-to-all-start.1 = ((bf16[4,32,512]{2,1,0:T(8,128)(2,1)}), bf16[4,32,512]{2,1,0:T(8,128)(2,1)S(1)}, u32[]{:S(2)}, u32[]{:S(2)}) async-start(bf16[4,32,512]{2,1,0:T(8,128)(2,1)} %copy.24), calls=%async_computation.1 | async-start | bytes 262144 | tf_op jit(solution)/shard_map/all_to_all | solution.py:38
  46.6 0.1 convert_reduce_fusion
  46.7 6.2 %all-to-all-done.1 = bf16[4,32,512]{2,1,0:T(8,128)(2,1)S(1)} async-done(((bf16[4,32,512]{2,1,0:T(8,128)(2,1)}), bf16[4,32,512]{2,1,0:T(8,128)(2,1)S(1)}, u32[]{:S(2)}, u32[]{:S(2)}) %all-to-all-start.1) | async-done | bytes 131104 | tf_op jit(solution)/shard_map/all_to_all | solution.py:38
  52.8 0.5 convolution_convert_fusion.1
  53.3 0.1 reshape.90
  53.4 0.2 copy.26
  53.6 0.1 copy.27
  53.7 3.7 %convolution_convert_fusion.2 = bf16[128,1024]{1,0:T(8,128)(2,1)} fusion(bf16[128,2048]{1,0:T(8,128)(2,1)S(1)} %bitcast.34, bf16[2048,1024]{1,0:T(8,128)(2,1)} %param.9), kind=kOutput, calls=%fused_computation.3 | convolution fusion | flops 537001984 | bytes 4980736 | tf_op jit(solution)/shard_map/dot_general | solution.py:54
  (8 shorter events, 0.0 us)
Async XLA Ops:
  6.5 28.8 %all-gather.3.cloned.1.call-start = ((), (), s32[]{:S(2)}) async-start(), calls=%async_computation.2 | async-start | bytes 1179648 | tf_op jit(solution)/shard_map/all_gather | solution.py:18
  9.4 32.5 %all-to-all-start = ((bf16[4,1,1]{2,1,0:T(2,128)(2,1)}), bf16[4,1,1]{2,1,0:T(2,128)(2,1)S(1)}, u32[]{:S(2)}, u32[]{:S(2)}) async-start(bf16[4,1,1]{2,1,0:T(2,128)(2,1)} %copy.20), calls=%async_computation | async-start | bytes 4096 | tf_op jit(solution)/shard_map/all_to_all | solution.py:39
  37.1 3.7 %copy-start = (s32[1,1,16]{2,1,0:T(1,128)S(1)}, s32[1,1,16]{2,1,0:T(1,128)}, u32[]{:S(2)}) copy-start(s32[1,1,16]{2,1,0:T(1,128)} %param.10) | copy-start | bytes 196
  41.9 10.9 %all-to-all-start.1 = ((bf16[4,32,512]{2,1,0:T(8,128)(2,1)}), bf16[4,32,512]{2,1,0:T(8,128)(2,1)S(1)}, u32[]{:S(2)}, u32[]{:S(2)}) async-start(bf16[4,32,512]{2,1,0:T(8,128)(2,1)} %copy.24), calls=%async_computation.1 | async-start | bytes 262144 | tf_op jit(solution)/shard_map/all_to_all | solution.py:38
Sparse Core Ops, SparseCore 0:
  9.2 26.0 all-gather.2
where the time goes:
time: 64.6 us; the launch traced here: 64.2 us
  waiting for transfers between devices  25.2 us (39%)
  between operations  13.5 us (21%)
  starting transfers between devices  11 us (17%)
  matrix products  7.44 us (12%)
  local copies, waits for them, and re-layouts  4.21 us (7%)
  other arithmetic  2.98 us (5%)
    all_gather x1, waiting for transfers between devices, on_device(): every = lax.all_gather(amplitudes[None], 'virt', axis=0, tiled=True)  18.3 us
    all_to_all x1, starting transfers between devices, on_device(): lax.all_to_all(output_marker, 'occ', split_axis=0, concat_axis=0, tiled=T...  6.35 us
    all_to_all x1, waiting for transfers between devices, on_device(): lax.all_to_all(outgoing, 'occ', split_axis=0, concat_axis=0, tiled=True)  6.18 us
    all_to_all x1, starting transfers between devices, on_device(): lax.all_to_all(outgoing, 'occ', split_axis=0, concat_axis=0, tiled=True)  4.6 us
    dot_general x1, matrix products, on_device(): jnp.dot(left, inter, preferred_element_type=jnp.float32)  3.65 us
    dot_general x1, matrix products, on_device(): jnp.dot(chosen_entries, integrals, preferred_element_type=jnp.float32)  2.93 us
    gather x1, local copies, waits for them, and re-layouts, on_device(): chosen_entries = jnp.take(every, panel_owner[0], axis=0)  1.79 us
  transfers between devices with their start and end apart: 3, of which 2 were waited for; matrix products, arithmetic and copies ran while one was open for 16% of the time, Pallas kernels for 0%

commit v1 on v0

--- a/solution.py
+++ b/solution.py
@@ -4,6 +4,21 @@
 from jax.sharding import PartitionSpec as P
 
 SROWS = 32
+
+
+def _write_strips_all(array_here, dim_at=0):
+    n_slots = lax.axis_size("virt")
+    before = [(i0 - 1, i0) for i0 in range(1, n_slots)] + [(n_slots - 1, 0)]
+    wide_out = array_here
+    history = [wide_out]
+    num = 0
+    while num < n_slots - 1:
+        wide_out = lax.ppermute(wide_out, "virt", before)
+        history += [wide_out]
+        num += 1
+    new = jnp.concatenate([*reversed(history)], dim_at)
+    taken_in = jnp.roll(new, (lax.axis_index("virt") + 1) * wide_out.shape[dim_at], dim_at)
+    return taken_in
 
 
 def on_device(amplitudes, integrals, panel_owner, inter, dest, screen):
@@ -15,7 +30,7 @@
     n_occ = lax.axis_size("occ")
     half_splits = op_rows // SROWS
     col_tiles = cols // tile
-    every = lax.all_gather(amplitudes[None], "virt", axis=0, tiled=True)
+    every = _write_strips_all(amplitudes[None])
     chosen_entries = jnp.take(every, panel_owner[0], axis=0)
     chosen_entries = chosen_entries.transpose(1, 0, 2).reshape(op_rows, steps * tile)
     accum = jnp.dot(chosen_entries, integrals, preferred_element_type=jnp.float32)

time: 64.6 us -> 61.8 us (0.957)
  between operations: 13.5 us -> 0.23 us
  waiting for transfers between devices: 25.2 us -> 35.3 us
    ppermute x0 -> x7, waiting for transfers between devices: none -> 29.5 us  [_write_strips_all(): wide_out = lax.ppermute(wide_out, 'virt', before)]
    all_gather x1 -> x0, waiting for transfers between devices: 18.3 us -> none  [on_device(): every = lax.all_gather(amplitudes[None], 'virt', axis=0, tiled=True)]
    unnamed x3 -> x20, local copies, waits for them, and re-layouts: 0.11 us -> 1.34 us
    gather x1, local copies, waits for them, and re-layouts: 1.79 us -> 0.56 us  [on_device(): chosen_entries = jnp.take(every, panel_owner[0], axis=0)]
    all_to_all x1, starting transfers between devices: 6.35 us -> 5.56 us  [on_device(): lax.all_to_all(output_marker, 'occ', split_axis=0, concat_axis=0, tiled=T...]
    unnamed x1 -> x0, waiting for transfers between devices: 0.71 us -> none
  transfers between devices with their start and end apart: 3 -> 9, of which waited for: 2 -> 7; matrix products, arithmetic and copies ran while one was open for 16% -> 16% of each run, Pallas kernels for 0% -> 0%
where the time goes in v1:
time: 61.8 us; the launch traced here: 61.4 us
  waiting for transfers between devices  35.3 us (57%)
  starting transfers between devices  11.2 us (18%)
  matrix products  7.44 us (12%)
  local copies, waits for them, and re-layouts  4.31 us (7%)
  other arithmetic  2.98 us (5%)
    ppermute x7, waiting for transfers between devices, _write_strips_all(): wide_out = lax.ppermute(wide_out, 'virt', before)  29.5 us
    all_to_all x1, waiting for transfers between devices, on_device(): lax.all_to_all(outgoing, 'occ', split_axis=0, concat_axis=0, tiled=True)  5.8 us
    all_to_all x1, starting transfers between devices, on_device(): lax.all_to_all(output_marker, 'occ', split_axis=0, concat_axis=0, tiled=T...  5.56 us
    all_to_all x1, starting transfers between devices, on_device(): lax.all_to_all(outgoing, 'occ', split_axis=0, concat_axis=0, tiled=True)  5.09 us
    dot_general x1, matrix products, on_device(): jnp.dot(left, inter, preferred_element_type=jnp.float32)  3.66 us
    dot_general x1, matrix products, on_device(): jnp.dot(chosen_entries, integrals, preferred_element_type=jnp.float32)  2.93 us
    unnamed x20, local copies, waits for them, and re-layouts  1.34 us
  transfers between devices with their start and end apart: 9, of which 7 were waited for; matrix products, arithmetic and copies ran while one was open for 16% of the time, Pallas kernels for 0%

profile of v1, /device:TPU:0, one launch (start us, length us, event | category | flops | bytes accessed | tf_op | source)
XLA Modules:
  0.0 61.4 jit_solution(15775541953678191858)
XLA Ops:
  0.0 0.5 collective-permute-start
  0.5 5.8 %collective-permute-done = bf16[1,128,512]{2,1,0:T(8,128)(2,1)S(1)} collective-permute-done((bf16[1,128,512]{2,1,0:T(8,128)(2,1)}, bf16[1,128,512]{2,1,0:T(8,128)(2,1)S(1)}, u32[]{:S(2)}, u32[]{:S(2)}) %collective-permute-start) | collective-permute-done | bytes 131104 | tf_op jit(solution)/shard_map/ppermute | solution.py:16
  6.3 5.3 %collective-permute-done.1 = bf16[1,128,512]{2,1,0:T(8,128)(2,1)S(1)} collective-permute-done((bf16[1,128,512]{2,1,0:T(8,128)(2,1)S(1)}, bf16[1,128,512]{2,1,0:T(8,128)(2,1)S(1)}, u32[]{:S(2)}, u32[]{:S(2)}) %collective-permute-start.1) | collective-permute-done | bytes 131104 | tf_op jit(solution)/shard_map/ppermute | solution.py:16
  11.6 0.7 %compare_bitcast_fusion = pred[16]{0:T(512)(128)(4,1)S(1)} fusion(s32[1,1,16]{2,1,0:T(1,128)} %param.11), kind=kLoop, calls=%fused_computation.35 | loop fusion | flops 16 | bytes 80 | tf_op jit(solution)/shard_map/eq | solution.py:45
  12.3 4.6 %collective-permute-done.2 = bf16[1,128,512]{2,1,0:T(8,128)(2,1)S(1)} collective-permute-done((bf16[1,128,512]{2,1,0:T(8,128)(2,1)S(1)}, bf16[1,128,512]{2,1,0:T(8,128)(2,1)S(1)}, u32[]{:S(2)}, u32[]{:S(2)}) %collective-permute-start.2) | collective-permute-done | bytes 131104 | tf_op jit(solution)/shard_map/ppermute | solution.py:16
  16.9 0.8 %select_reduce_fusion = s32[4]{0:T(128)S(1)} fusion(s32[16]{0:T(128)S(1)} %iota_add_fusion, s32[16]{0:T(128)} %bitcast.41, pred[16]{0:T(512)(128)(4,1)S(1)} %compare_bitcast_fusion), kind=kLoop, calls=%fused_computation.28 | loop fusion | flops 252 | bytes 160 | tf_op jit(solution)/shard_map/reduce_sum | solution.py:49
  17.7 4.5 %collective-permute-done.3 = bf16[1,128,512]{2,1,0:T(8,128)(2,1)S(1)} collective-permute-done((bf16[1,128,512]{2,1,0:T(8,128)(2,1)S(1)}, bf16[1,128,512]{2,1,0:T(8,128)(2,1)S(1)}, u32[]{:S(2)}, u32[]{:S(2)}) %collective-permute-start.3) | collective-permute-done | bytes 131104 | tf_op jit(solution)/shard_map/ppermute | solution.py:16
  22.2 0.7 %copy.20 = bf16[4,1,1]{2,1,0:T(2,128)(2,1)} copy(bf16[4,1,1]{0,2,1:T(2,128)(2,1)S(1)} %convert_bitcast_fusion) | data formatting | bytes 16 | tf_op jit(solution)/shard_map/convert_element_type | solution.py:49
  22.9 5.6 %all-to-all-start = ((bf16[4,1,1]{2,1,0:T(2,128)(2,1)}), bf16[4,1,1]{2,1,0:T(2,128)(2,1)S(1)}, u32[]{:S(2)}, u32[]{:S(2)}) async-start(bf16[4,1,1]{2,1,0:T(2,128)(2,1)} %copy.20), calls=%async_computation | async-start | bytes 4096 | tf_op jit(solution)/shard_map/all_to_all | solution.py:54
  28.4 0.7 %fusion.11 = s32[2]{0:T(128)S(1)} fusion(s32[1,2]{1,0:T(1,128)} %param.8), kind=kLoop, calls=%fused_computation.40 | loop fusion | flops 6 | bytes 16 | tf_op jit(solution)/shard_map/jit(_take)/jit(_where)/select_n | solution.py:34
  29.1 4.6 %collective-permute-done.5 = bf16[1,128,512]{2,1,0:T(8,128)(2,1)S(1)} collective-permute-done((bf16[1,128,512]{2,1,0:T(8,128)(2,1)S(1)}, bf16[1,128,512]{2,1,0:T(8,128)(2,1)S(1)}, u32[]{:S(2)}, u32[]{:S(2)}) %collective-permute-start.5) | collective-permute-done | bytes 131104 | tf_op jit(solution)/shard_map/ppermute | solution.py:16
  33.7 0.7 %compare_and_fusion = pred[2]{0:T(512)(128)(4,1)S(1)} fusion(s32[1,2]{1,0:T(1,128)} %param.8), kind=kLoop, calls=%fused_computation.33 | loop fusion | flops 12 | bytes 10 | tf_op jit(solution)/shard_map/jit(_take)/and | solution.py:34
  34.4 4.6 %collective-permute-done.6 = bf16[1,128,512]{2,1,0:T(8,128)(2,1)S(1)} collective-permute-done((bf16[1,128,512]{2,1,0:T(8,128)(2,1)S(1)}, bf16[1,128,512]{2,1,0:T(8,128)(2,1)S(1)}, u32[]{:S(2)}, u32[]{:S(2)}) %collective-permute-start.6) | collective-permute-done | bytes 131104 | tf_op jit(solution)/shard_map/ppermute | solution.py:16
  39.1 0.9 %constant_dynamic-update-slice_fusion.8 = bf16[16,128,512]{2,1,0:T(8,128)(2,1)S(1)} fusion(bf16[16,128,512]{2,1,0:T(8,128)(2,1)S(1)} %constant_dynamic-update-slice_fusion.9, bf16[128,512]{1,0:T(8,128)(2,1)} %param.6), kind=kLoop, calls=%fused_computation.16 | loop fusion | bytes 262144
  40.3 0.6 gather_fusion
  41.2 2.9 %convolution_convert_fusion = bf16[128,2048]{1,0:T(8,128)(2,1)S(1)} fusion(bf16[128,1024]{0,1:T(8,128)(2,1)S(1)} %bitcast.39, bf16[1024,2048]{1,0:T(8,128)(2,1)} %param.7), kind=kOutput, calls=%fused_computation.1 | convolution fusion | flops 537133056 | bytes 4980736 | tf_op jit(solution)/shard_map/dot_general | solution.py:36
  44.1 0.4 reshape.88
  44.8 0.4 convolution_convert_fusion.3
  45.2 0.7 %copy.24 = bf16[4,32,512]{2,1,0:T(8,128)(2,1)} copy(bf16[4,32,512]{2,0,1:T(4,128)(2,1)S(1)} %convolution_convert_fusion.3) | data formatting | bytes 262144 | tf_op jit(solution)/shard_map/convert_element_type | solution.py:48
  45.8 5.1 %all-to-all-start.1 = ((bf16[4,32,512]{2,1,0:T(8,128)(2,1)}), bf16[4,32,512]{2,1,0:T(8,128)(2,1)S(1)}, u32[]{:S(2)}, u32[]{:S(2)}) async-start(bf16[4,32,512]{2,1,0:T(8,128)(2,1)} %copy.24), calls=%async_computation.1 | async-start | bytes 262144 | tf_op jit(solution)/shard_map/all_to_all | solution.py:53
  51.1 5.8 %all-to-all-done.1 = bf16[4,32,512]{2,1,0:T(8,128)(2,1)S(1)} async-done(((bf16[4,32,512]{2,1,0:T(8,128)(2,1)}), bf16[4,32,512]{2,1,0:T(8,128)(2,1)S(1)}, u32[]{:S(2)}, u32[]{:S(2)}) %all-to-all-start.1) | async-done | bytes 131104 | tf_op jit(solution)/shard_map/all_to_all | solution.py:53
  56.9 0.5 convolution_convert_fusion.1
  57.4 0.2 copy.26
  57.7 3.7 %convolution_convert_fusion.2 = bf16[128,1024]{1,0:T(8,128)(2,1)} fusion(bf16[128,2048]{1,0:T(8,128)(2,1)S(1)} %bitcast.36, bf16[2048,1024]{1,0:T(8,128)(2,1)} %param.9), kind=kOutput, calls=%fused_computation.3 | convolution fusion | flops 537001984 | bytes 4980736 | tf_op jit(solution)/shard_map/dot_general | solution.py:69
  (38 shorter events, 1.1 us)
Async XLA Ops:
  0.0 40.2 %copy-start = (bf16[128,512]{1,0:T(8,128)(2,1)S(1)}, bf16[128,512]{1,0:T(8,128)(2,1)}, u32[]{:S(2)}) copy-start(bf16[128,512]{1,0:T(8,128)(2,1)} %param.6) | copy-start | bytes 393220
  0.0 6.3 %collective-permute-start = (bf16[1,128,512]{2,1,0:T(8,128)(2,1)}, bf16[1,128,512]{2,1,0:T(8,128)(2,1)S(1)}, u32[]{:S(2)}, u32[]{:S(2)}) collective-permute-start(bf16[1,128,512]{2,1,0:T(8,128)(2,1)} %bitcast.40), channel_id=1, source_target_pairs={{0,4},{4,8},{8,12},{12,16},{16,20},{20,24},{24,28},{28,0},{1,5},{5... | collective-permute-start | bytes 393224 | tf_op jit(solution)/shard_map/ppermute | solution.py:16
  6.3 5.3 %collective-permute-start.1 = (bf16[1,128,512]{2,1,0:T(8,128)(2,1)S(1)}, bf16[1,128,512]{2,1,0:T(8,128)(2,1)S(1)}, u32[]{:S(2)}, u32[]{:S(2)}) collective-permute-start(bf16[1,128,512]{2,1,0:T(8,128)(2,1)S(1)} %collective-permute-done), channel_id=1, source_target_pairs={{0,4},{4,8},{8,12},{12,16},{16,20},{20,24},{24,28},{28,0},{1,5},{5... | collective-permute-start | bytes 393224 | tf_op jit(solution)/shard_map/ppermute | solution.py:16
  11.6 5.3 %collective-permute-start.2 = (bf16[1,128,512]{2,1,0:T(8,128)(2,1)S(1)}, bf16[1,128,512]{2,1,0:T(8,128)(2,1)S(1)}, u32[]{:S(2)}, u32[]{:S(2)}) collective-permute-start(bf16[1,128,512]{2,1,0:T(8,128)(2,1)S(1)} %collective-permute-done.1), channel_id=1, source_target_pairs={{0,4},{4,8},{8,12},{12,16},{16,20},{20,24},{24,28},{28,0},{1,5},{5... | collective-permute-start | bytes 393224 | tf_op jit(solution)/shard_map/ppermute | solution.py:16
  16.9 5.3 %collective-permute-start.3 = (bf16[1,128,512]{2,1,0:T(8,128)(2,1)S(1)}, bf16[1,128,512]{2,1,0:T(8,128)(2,1)S(1)}, u32[]{:S(2)}, u32[]{:S(2)}) collective-permute-start(bf16[1,128,512]{2,1,0:T(8,128)(2,1)S(1)} %collective-permute-done.2), channel_id=1, source_target_pairs={{0,4},{4,8},{8,12},{12,16},{16,20},{20,24},{24,28},{28,0},{1,5},{5... | collective-permute-start | bytes 393224 | tf_op jit(solution)/shard_map/ppermute | solution.py:16
  22.2 6.3 %collective-permute-start.4 = (bf16[1,128,512]{2,1,0:T(8,128)(2,1)S(1)}, bf16[1,128,512]{2,1,0:T(8,128)(2,1)S(1)}, u32[]{:S(2)}, u32[]{:S(2)}) collective-permute-start(bf16[1,128,512]{2,1,0:T(8,128)(2,1)S(1)} %collective-permute-done.3), channel_id=1, source_target_pairs={{0,4},{4,8},{8,12},{12,16},{16,20},{20,24},{24,28},{28,0},{1,5},{5... | collective-permute-start | bytes 393224 | tf_op jit(solution)/shard_map/ppermute | solution.py:16
  22.9 23.0 %all-to-all-start = ((bf16[4,1,1]{2,1,0:T(2,128)(2,1)}), bf16[4,1,1]{2,1,0:T(2,128)(2,1)S(1)}, u32[]{:S(2)}, u32[]{:S(2)}) async-start(bf16[4,1,1]{2,1,0:T(2,128)(2,1)} %copy.20), calls=%async_computation | async-start | bytes 4096 | tf_op jit(solution)/shard_map/all_to_all | solution.py:54
  28.4 5.3 %collective-permute-start.5 = (bf16[1,128,512]{2,1,0:T(8,128)(2,1)S(1)}, bf16[1,128,512]{2,1,0:T(8,128)(2,1)S(1)}, u32[]{:S(2)}, u32[]{:S(2)}) collective-permute-start(bf16[1,128,512]{2,1,0:T(8,128)(2,1)S(1)} %collective-permute-done.4), channel_id=1, source_target_pairs={{0,4},{4,8},{8,12},{12,16},{16,20},{20,24},{24,28},{28,0},{1,5},{5... | collective-permute-start | bytes 393224 | tf_op jit(solution)/shard_map/ppermute | solution.py:16
  33.7 5.3 %collective-permute-start.6 = (bf16[1,128,512]{2,1,0:T(8,128)(2,1)S(1)}, bf16[1,128,512]{2,1,0:T(8,128)(2,1)S(1)}, u32[]{:S(2)}, u32[]{:S(2)}) collective-permute-start(bf16[1,128,512]{2,1,0:T(8,128)(2,1)S(1)} %collective-permute-done.5), channel_id=1, source_target_pairs={{0,4},{4,8},{8,12},{12,16},{16,20},{20,24},{24,28},{28,0},{1,5},{5... | collective-permute-start | bytes 393224 | tf_op jit(solution)/shard_map/ppermute | solution.py:16
  44.1 0.7 %copy-start.1 = (s32[1,1,16]{2,1,0:T(1,128)S(1)}, s32[1,1,16]{2,1,0:T(1,128)}, u32[]{:S(2)}) copy-start(s32[1,1,16]{2,1,0:T(1,128)} %param.10) | copy-start | bytes 196
  45.8 11.0 %all-to-all-start.1 = ((bf16[4,32,512]{2,1,0:T(8,128)(2,1)}), bf16[4,32,512]{2,1,0:T(8,128)(2,1)S(1)}, u32[]{:S(2)}, u32[]{:S(2)}) async-start(bf16[4,32,512]{2,1,0:T(8,128)(2,1)} %copy.24), calls=%async_computation.1 | async-start | bytes 262144 | tf_op jit(solution)/shard_map/all_to_all | solution.py:53
